TPU v7x, 32 devices: a whole 2x2x4 slice. The times are simulated.
32 devices in a mesh: rows: 4 (over y, x), cols: 8 (over z, core).
Axes of the slice: x: 2, y: 2, z: 4, core: 2. Of those that a mesh axis runs over, the one named last changes fastest.
Arguments:
- tokens: bfloat16 [128, 256, 256], P('rows', 'cols'), may hold values from -45 to 45
- key_bias: bfloat16 [128, 256], P('rows', 'cols'), may hold values from -3 to 250
- cotangent: bfloat16 [128, 256, 256], P('rows', 'cols'), may hold values from -6 to 6
- gain_row: float32 [256], replicated, may hold values from 0.1 to 1.9
- w_qkv_row: bfloat16 [256, 768], replicated, may hold values from -0.375 to 0.375
- w_out_row: bfloat16 [256, 256], replicated, may hold values from -0.375 to 0.375
- gain_col: float32 [256], replicated, may hold values from 0.1 to 1.9
- w_qkv_col: bfloat16 [256, 768], replicated, may hold values from -0.375 to 0.375
- w_out_col: bfloat16 [256, 256], replicated, may hold values from -0.375 to 0.375
- gain_mlp: float32 [256], replicated, may hold values from 0.1 to 1.9
- w_up: bfloat16 [256, 1024], replicated, may hold values from -0.375 to 0.375
- w_down: bfloat16 [1024, 256], replicated, may hold values from -0.1875 to 0.1875
Outputs:
- d_tokens: bfloat16 [128, 256, 256], P('rows', 'cols')
- d_gain_row: float32 [256], replicated
- d_w_qkv_row: float32 [256, 768], replicated
- d_w_out_row: float32 [256, 256], replicated
- d_gain_col: float32 [256], replicated
- d_w_qkv_col: float32 [256, 768], replicated
- d_w_out_col: float32 [256, 256], replicated
- d_gain_mlp: float32 [256], replicated
- d_w_up: float32 [256, 1024], replicated
- d_w_down: float32 [1024, 256], replicated
All inputs are finite; a program needn't handle non-finite values.
Results may differ from a plain program's by a relative error of at most 0.015.
Values may be sent and summed in bfloat16 or wider, within the bound.
No kernel may reach another device: no remote copies, remote signals or barrier semaphores. Data moves between devices by JAX's collectives and lax.ppermute only.
A program may use at most 128 MiB of HBM per device.

v0:
```python
import jax
import jax.numpy as jnp
from jax import lax
from jax.sharding import PartitionSpec as P

HEADS = 4


def product(spec_text, left_op, right_op):
    return jnp.einsum(spec_text, left_op, right_op, preferred_element_type=jnp.float32)


def layer_norm(entries, gain_vec):
    floats = entries.astype(jnp.float32)
    centred = floats - jnp.mean(floats, axis=-1, keepdims=True)
    inverse = lax.rsqrt(jnp.mean(centred * centred, axis=-1, keepdims=True) + 1e-05)
    normed = centred * inverse
    return ((normed * gain_vec).astype(jnp.bfloat16), normed, inverse)


def norm_back(grad_out, normed, inverse, gain_vec):
    scaled = grad_out * gain_vec
    result = inverse * (
        scaled
        - jnp.mean(scaled, axis=-1, keepdims=True)
        - normed * jnp.mean(scaled * normed, axis=-1, keepdims=True)
    )
    gain_grad = jnp.sum((grad_out * normed).reshape(-1, gain_vec.shape[0]), axis=0)
    return (result, gain_grad)


def over_cells(left_op, right_op):
    left_flat = left_op.reshape(-1, left_op.shape[-1])
    right_flat = right_op.reshape(-1, right_op.shape[-1])
    return lax.dot_general(
        left_flat, right_flat, (((0,), (0,)), ((), ())), preferred_element_type=jnp.float32
    )


def times_transpose(entries, weight):
    return lax.dot_general(
        entries, weight, (((entries.ndim - 1,), (1,)), ((), ())), preferred_element_type=jnp.float32
    )


def letters(length_axis):
    if length_axis == 1:
        return ("sqhd,skhd->shqk", "shqk,skhd->sqhd", "shqk,sqhd->skhd")
    return ("qshd,kshd->shqk", "shqk,kshd->qshd", "shqk,qshd->kshd")


def split_heads(packed, head_count):
    features = packed.shape[-1] // 3
    head_shape = packed.shape[:-1] + (head_count, features // head_count)
    return tuple(
        (
            packed[..., member * features : (member + 1) * features].reshape(head_shape)
            for member in range(3)
        )
    )


def key_terms(bias_rows, length_axis):
    floats = bias_rows.astype(jnp.float32)
    if length_axis == 0:
        floats = floats.T
    return floats[:, None, None, :]


def attention_weights(query_block, key_rows, bias_terms, factor, length_axis):
    scores = product(letters(length_axis)[0], query_block, key_rows) * factor + bias_terms
    shifted = jnp.exp(scores - jnp.max(scores, axis=-1, keepdims=True))
    return shifted / jnp.sum(shifted, axis=-1, keepdims=True)


def join_blocks(stacked, length_axis, features):
    if length_axis == 0:
        return stacked.reshape((-1, stacked.shape[2], features))
    reordered = jnp.moveaxis(stacked, 0, 1)
    return reordered.reshape((reordered.shape[0], -1, features))


def attend(packed, bias_rows, head_count, length_axis):
    query_rows, key_rows, value_rows = split_heads(packed, head_count)
    length = packed.shape[length_axis]
    block_len = min(length, 512)
    factor = query_rows.shape[-1] ** (-0.5)
    bias_terms = key_terms(bias_rows, length_axis)
    mixing = letters(length_axis)[1]

    def one_block(offset):
        query_block = lax.dynamic_slice_in_dim(query_rows, offset, block_len, length_axis)
        weights = attention_weights(query_block, key_rows, bias_terms, factor, length_axis)
        return product(mixing, weights.astype(jnp.bfloat16), value_rows).astype(jnp.bfloat16)

    offsets = jnp.arange(length // block_len, dtype=jnp.int32) * block_len
    return join_blocks(lax.map(one_block, offsets), length_axis, packed.shape[-1] // 3)


def attend_back(grad_out, packed, bias_rows, head_count, length_axis):
    query_rows, key_rows, value_rows = split_heads(packed, head_count)
    features = packed.shape[-1] // 3
    grad_heads = grad_out.reshape(query_rows.shape)
    length = packed.shape[length_axis]
    block_len = min(length, 512)
    factor = query_rows.shape[-1] ** (-0.5)
    bias_terms = key_terms(bias_rows, length_axis)
    score_spec, mixing, gather_spec = letters(length_axis)

    def one_block(running, offset):
        key_grad, value_grad = running
        query_block = lax.dynamic_slice_in_dim(query_rows, offset, block_len, length_axis)
        grad_block = lax.dynamic_slice_in_dim(grad_heads, offset, block_len, length_axis)
        weights = attention_weights(query_block, key_rows, bias_terms, factor, length_axis)
        weights_low = weights.astype(jnp.bfloat16)
        weight_grad = product(score_spec, grad_block, value_rows)
        centre = jnp.sum(weights * weight_grad, axis=-1, keepdims=True)
        score_grad = (weights * (weight_grad - centre) * factor).astype(jnp.bfloat16)
        query_grad = product(mixing, score_grad, key_rows)
        key_grad = key_grad + product(gather_spec, score_grad, query_block)
        value_grad = value_grad + product(gather_spec, weights_low, grad_block)
        return ((key_grad, value_grad), query_grad)

    empty_grad = jnp.zeros(key_rows.shape, jnp.float32)
    offsets = jnp.arange(length // block_len, dtype=jnp.int32) * block_len
    (key_grad, value_grad), query_parts = lax.scan(one_block, (empty_grad, empty_grad), offsets)
    query_grad = join_blocks(query_parts, length_axis, features)
    flat_shape = packed.shape[:-1] + (features,)
    joined = jnp.concatenate(
        [query_grad, key_grad.reshape(flat_shape), value_grad.reshape(flat_shape)], axis=-1
    )
    return joined.astype(jnp.bfloat16)


def attention_forward(inputs, bias_rows, gain_vec, w_qkv, w_out, head_count, length_axis):
    normal_in, normed, inverse = layer_norm(inputs, gain_vec)
    packed = jnp.dot(normal_in, w_qkv, preferred_element_type=jnp.float32).astype(jnp.bfloat16)
    mixed_out = attend(packed, bias_rows, head_count, length_axis)
    output = (
        inputs.astype(jnp.float32) + jnp.dot(mixed_out, w_out, preferred_element_type=jnp.float32)
    ).astype(jnp.bfloat16)
    return (output, (normal_in, normed, inverse, packed, mixed_out))


def attention_backward(
    grad_out, saved_parts, bias_rows, gain_vec, w_qkv, w_out, head_count, length_axis
):
    normal_in, normed, inverse, packed, mixed_out = saved_parts
    out_grad = over_cells(mixed_out, grad_out)
    mixed_grad = times_transpose(grad_out, w_out).astype(jnp.bfloat16)
    packed_grad = attend_back(mixed_grad, packed, bias_rows, head_count, length_axis)
    qkv_grad = over_cells(normal_in, packed_grad)
    input_grad, gain_grad = norm_back(
        times_transpose(packed_grad, w_qkv), normed, inverse, gain_vec
    )
    return (
        (grad_out.astype(jnp.float32) + input_grad).astype(jnp.bfloat16),
        (gain_grad, qkv_grad, out_grad),
    )


def feed_backward(inputs, grad_out, gain_vec, w_up, w_down):
    normal_in, normed, inverse = layer_norm(inputs, gain_vec)
    hidden = jnp.dot(normal_in, w_up, preferred_element_type=jnp.float32)
    active, gelu_back = jax.vjp(jax.nn.gelu, hidden)
    active_low = active.astype(jnp.bfloat16)
    down_grad = over_cells(active_low, grad_out)
    hidden_grad = gelu_back(times_transpose(grad_out, w_down))[0].astype(jnp.bfloat16)
    up_grad = over_cells(normal_in, hidden_grad)
    input_grad, gain_grad = norm_back(times_transpose(hidden_grad, w_up), normed, inverse, gain_vec)
    return (
        (grad_out.astype(jnp.float32) + input_grad).astype(jnp.bfloat16),
        (gain_grad, up_grad, down_grad),
    )


def shards(
    tokens,
    key_bias,
    cotangent,
    gain_row,
    w_qkv_row,
    w_out_row,
    gain_col,
    w_qkv_col,
    w_out_col,
    gain_mlp,
    w_up,
    w_down,
):
    row_cells, row_bias = (
        lax.all_to_all(tokens, "cols", split_axis=0, concat_axis=1, tiled=True),
        lax.all_to_all(key_bias, "cols", split_axis=0, concat_axis=1, tiled=True),
    )
    after_rows, row_saved = attention_forward(
        row_cells, row_bias, gain_row, w_qkv_row, w_out_row, HEADS, 1
    )
    column_cells = lax.all_to_all(
        lax.all_to_all(after_rows, "cols", split_axis=1, concat_axis=0, tiled=True),
        "rows",
        split_axis=1,
        concat_axis=0,
        tiled=True,
    )
    column_grads, column_bias = (
        lax.all_to_all(cotangent, "rows", split_axis=1, concat_axis=0, tiled=True),
        lax.all_to_all(key_bias, "rows", split_axis=1, concat_axis=0, tiled=True),
    )
    after_cols, column_saved = attention_forward(
        column_cells, column_bias, gain_col, w_qkv_col, w_out_col, HEADS, 0
    )
    mid_grad, feed_grads = feed_backward(after_cols, column_grads, gain_mlp, w_up, w_down)
    cell_grad, attn_grads = attention_backward(
        mid_grad, column_saved, column_bias, gain_col, w_qkv_col, w_out_col, HEADS, 0
    )
    factor = float(
        tokens.shape[0] * tokens.shape[1] * lax.axis_size("rows") * lax.axis_size("cols")
    ) ** (-0.5)
    other_sums = tuple((grad_term * factor for grad_term in attn_grads + feed_grads))
    grad_rows = lax.all_to_all(
        lax.all_to_all(cell_grad, "rows", split_axis=0, concat_axis=1, tiled=True),
        "cols",
        split_axis=0,
        concat_axis=1,
        tiled=True,
    )
    token_grad_rows, row_grads = attention_backward(
        grad_rows, row_saved, row_bias, gain_row, w_qkv_row, w_out_row, HEADS, 1
    )
    d_tokens = lax.all_to_all(token_grad_rows, "cols", split_axis=1, concat_axis=0, tiled=True)
    row_sums = tuple((grad_term * factor for grad_term in row_grads))
    summed = lax.psum(
        (
            row_sums[0],
            row_sums[1],
            row_sums[2],
            other_sums[0],
            other_sums[1],
            other_sums[2],
            other_sums[3],
            other_sums[4],
            other_sums[5],
        ),
        ("rows", "cols"),
    )
    row_sums = summed[:3]
    other_sums = summed[3:]
    return (
        d_tokens,
        row_sums[0],
        row_sums[1],
        row_sums[2],
        other_sums[0],
        other_sums[1],
        other_sums[2],
        other_sums[3],
        other_sums[4],
        other_sums[5],
    )


def solution(mesh):
    in_specs = (
        P("rows", "cols", None),
        P("rows", "cols"),
        P("rows", "cols", None),
        P(),
        P(),
        P(),
        P(),
        P(),
        P(),
        P(),
        P(),
        P(),
    )
    out_specs = (P("rows", "cols", None), P(), P(), P(), P(), P(), P(), P(), P(), P())
    return jax.shard_map(shards, mesh=mesh, in_specs=in_specs, out_specs=out_specs, check_vma=False)
```

profile of v0, /device:TPU:0, one launch (start us, length us, event | category | flops | bytes accessed | tf_op | source)
XLA Modules:
  0.0 385.8 jit_solution(3843586543527307721)
XLA Ops:
  7.2 12.1 %all_to_all.134 = bf16[8,4,32]{2,1,0:T(4,128)(2,1)S(1)} all-to-all(bf16[8,4,32]{2,1,0:T(4,128)(2,1)} %bitcast.263), channel_id=1, replica_groups=mesh['rows'=4,'cols'=8] {'cols'}, dimensions={0} | all-to-all | bytes 4096 | tf_op jit(solution)/shard_map/all_to_all | solution.py:193
  19.3 3.6 all-to-all-start.1
  24.4 13.7 %all-to-all-done.1 = bf16[32,32,256]{2,1,0:T(8,128)(2,1)S(1)} async-done(((bf16[32,32,256]{2,1,0:T(8,128)(2,1)}), bf16[32,32,256]{2,1,0:T(8,128)(2,1)S(1)}, u32[]{:S(2)}, u32[]{:S(2)}) %all-to-all-start.1) | async-done | bytes 524320 | tf_op jit(solution)/shard_map/all_to_all | solution.py:192
  38.2 3.7 all-to-all-start.5
  46.3 4.7 %fusion.124 = (f32[4,4,256]{2,1,0:T(4,128)S(1)}, f32[4,4,256,256]{2,3,1,0:T(8,128)}) fusion(f32[4,256]{1,0:T(4,128)S(1)} %reshape.252, bf16[4,256,4,64]{1,3,2,0:T(8,128)(2,1)S(1)} %bitcast.249, bf16[4,256,4,64]{1,3,2,0:T(8,128)(2,1)} %bitcast.247), kind=kOutput, calls=%fused_computation.165 | convolution fusion | flops 138412288 | bytes 5263360 | tf_op jit(solution)/shard_map/while/body/eval_jaxpr/sub | solution.py:72
  51.0 2.7 convolution_convert_fusion.7
  56.1 3.5 all-to-all-start.3
  60.7 14.2 %all-to-all-done.3 = bf16[4,256,256]{2,0,1:T(4,128)(2,1)S(1)} async-done(((bf16[4,256,256]{2,0,1:T(4,128)(2,1)}), bf16[4,256,256]{2,0,1:T(4,128)(2,1)S(1)}, u32[]{:S(2)}, u32[]{:S(2)}) %all-to-all-start.3) | async-done | bytes 524320 | tf_op jit(solution)/shard_map/all_to_all | solution.py:199
  74.8 4.2 %all-to-all-start = ((bf16[32,32,256]{2,0,1:T(8,128)(2,1)}), bf16[32,32,256]{2,0,1:T(8,128)(2,1)S(1)}, u32[]{:S(2)}, u32[]{:S(2)}) async-start(bf16[32,32,256]{2,0,1:T(8,128)(2,1)} %copy.364), calls=%async_computation | async-start | bytes 1048576 | tf_op jit(solution)/shard_map/all_to_all | solution.py:206
  80.2 6.6 %all-to-all-done = bf16[32,32,256]{2,0,1:T(8,128)(2,1)S(1)} async-done(((bf16[32,32,256]{2,0,1:T(8,128)(2,1)}), bf16[32,32,256]{2,0,1:T(8,128)(2,1)S(1)}, u32[]{:S(2)}, u32[]{:S(2)}) %all-to-all-start) | async-done | bytes 524320 | tf_op jit(solution)/shard_map/all_to_all | solution.py:206
  86.9 3.7 all-to-all-start.4
  91.5 5.8 %all-to-all-done.4 = bf16[32,32,256]{2,0,1:T(8,128)(2,1)S(1)} async-done(((bf16[32,32,256]{2,0,1:T(8,128)(2,1)}), bf16[32,32,256]{2,0,1:T(8,128)(2,1)S(1)}, u32[]{:S(2)}, u32[]{:S(2)}) %all-to-all-start.4) | async-done | bytes 524320 | tf_op jit(solution)/shard_map/all_to_all | solution.py:198
  107.9 3.7 fusion.125
  115.3 2.8 multiply_convert_fusion
  118.2 3.2 fusion.10
  127.3 3.5 convolution_convert_fusion.5
  132.6 5.2 %fusion.42 = bf16[8,4,64,128]{3,2,1,0:T(8,128)(2,1)} fusion(bf16[128,8,4,64]{0,3,2,1:T(8,128)(2,1)} %bitcast.252, f32[8,4,128,128]{2,3,1,0:T(8,128)} %fusion.126, f32[8,4,128,128]{2,3,1,0:T(8,128)} %get-tuple-element.127, f32[8,4,128]{2,1,0:T(4,128)S(1)} %get-tuple-element.126), kind=kOutput, calls=%fused_computation.49 | convolution fusion | flops 71045248 | bytes 5259264 | tf_op jit(solution)/shard_map/while/body/eval_jaxpr/shqk,kshd->qshd/dot_general | solution.py:10
  137.9 5.0 %fusion.45 = bf16[8,4,64,128]{3,2,1,0:T(8,128)(2,1)} fusion(bf16[128,8,4,64]{0,3,2,1:T(8,128)(2,1)S(1)} %bitcast.254, f32[8,4,128,128]{2,3,1,0:T(8,128)} %fusion.126, f32[8,4,128,128]{2,3,1,0:T(8,128)} %get-tuple-element.127, f32[8,4,128]{2,1,0:T(4,128)S(1)} %get-tuple-element.126), kind=kOutput, calls=%fused_computation.50 | convolution fusion | flops 71045248 | bytes 5259264 | tf_op jit(solution)/shard_map/while/body/eval_jaxpr/shqk,qshd->kshd/dot_general | solution.py:10
  148.4 3.2 multiply_reduce_fusion.2
  153.6 4.1 %all-to-all-start.6 = ((bf16[128,8,256]{2,1,0:T(8,128)(2,1)}), bf16[128,8,256]{2,1,0:T(8,128)(2,1)}, u32[]{:S(2)}, u32[]{:S(2)}) async-start(bf16[128,8,256]{2,1,0:T(8,128)(2,1)} %copy.399), calls=%async_computation.6 | async-start | bytes 1048576 | tf_op jit(solution)/shard_map/all_to_all | solution.py:221
  166.3 3.5 all-to-all-start.7
  172.3 3.0 fusion.56
  177.3 2.4 fusion.39
  179.7 5.3 %all-to-all-done.7 = bf16[32,32,256]{2,1,0:T(8,128)(2,1)S(1)} async-done(((bf16[32,32,256]{2,1,0:T(8,128)(2,1)}), bf16[32,32,256]{2,1,0:T(8,128)(2,1)S(1)}, u32[]{:S(2)}, u32[]{:S(2)}) %all-to-all-start.7) | async-done | bytes 524320 | tf_op jit(solution)/shard_map/all_to_all | solution.py:220
  185.4 3.8 convolution_convert_fusion.4
  189.3 2.7 fusion.127
  192.0 8.0 %fusion.48 = bf16[4,4,64,256]{3,2,1,0:T(8,128)(2,1)} fusion(bf16[4,256,4,64]{1,3,2,0:T(8,128)(2,1)S(1)} %bitcast.248, f32[4,4,256,256]{2,3,1,0:T(8,128)} %fusion.127, f32[4,4,256,256]{2,3,1,0:T(8,128)} %get-tuple-element.125, f32[4,4,256]{2,1,0:T(4,128)S(1)} %get-tuple-element.124), kind=kOutput, calls=%fused_computation.51 | convolution fusion | flops 141824256 | bytes 9453568 | tf_op jit(solution)/shard_map/while/body/eval_jaxpr/shqk,skhd->sqhd/dot_general | solution.py:10
  200.0 8.0 %fusion.51 = bf16[4,4,64,256]{3,2,1,0:T(8,128)(2,1)} fusion(bf16[4,256,4,64]{1,3,2,0:T(8,128)(2,1)S(1)} %bitcast.250, f32[4,4,256,256]{2,3,1,0:T(8,128)} %fusion.127, f32[4,4,256,256]{2,3,1,0:T(8,128)} %get-tuple-element.125, f32[4,4,256]{2,1,0:T(4,128)S(1)} %get-tuple-element.124), kind=kOutput, calls=%fused_computation.52 | convolution fusion | flops 141824256 | bytes 9453568 | tf_op jit(solution)/shard_map/while/body/eval_jaxpr/shqk,sqhd->skhd/dot_general | solution.py:10
  214.5 2.7 fusion.57
  221.9 3.5 all-to-all-start.8
  225.4 41.2 %all-reduce = (f32[256]{0:T(256)}, f32[256]{0:T(256)}, f32[256]{0:T(256)}) all-reduce(f32[256]{0:T(256)S(1)} %broadcast_multiply_fusion.11, f32[256]{0:T(256)S(1)} %broadcast_multiply_fusion.10, f32[256]{0:T(256)S(1)} %broadcast_multiply_fusion.9), channel_id=1, replica_groups=mesh['rows'=4,'cols'=8] {'rows','cols'}, use_global_device_ids=true, to_apply=%region_19.20 | all-reduce | flops 768 | bytes 6144 | tf_op jit(solution)/shard_map/psum | solution.py:232
  267.6 102.7 %all-reduce.4.cloned.1.call-done = (f32[256,768]{1,0:T(8,128)}, f32[256,256]{1,0:T(8,128)}, f32[256,768]{1,0:T(8,128)}, f32[256,256]{1,0:T(8,128)}, f32[256,1024]{1,0:T(8,128)}, /*index=5*/f32[1024,256]{1,0:T(8,128)}) async-done(((f32[256,768]{1,0:T(8,128)}, f32[256,256]{1,0:T(8,128)}, f32[256,768]{1,0:T(8,128)}, f32[256,256]{1,0:T(8,128)}, f32[256,1024]{1,0:T(8,128)}, /*index=5*/f32[1024,256]{1,0:T(8,128)}), ...) | async-done | bytes 4194320 | tf_op jit(solution)/shard_map/psum | solution.py:232
  (194 shorter events, 75.1 us)
Async XLA Ops:
  7.2 108.1 %copy-start = (bf16[256,1024]{1,0:T(8,128)(2,1)S(1)}, bf16[256,1024]{1,0:T(8,128)(2,1)}, u32[]{:S(2)}) copy-start(bf16[256,1024]{1,0:T(8,128)(2,1)} %param.22) | copy-start | bytes 1572868
  19.3 23.7 %copy-start.41 = (f32[256]{0:T(256)S(1)}, f32[256]{0:T(256)}, u32[]{:S(2)}) copy-start(f32[256]{0:T(256)} %param.15) | copy-start | bytes 3076
  19.3 18.9 %all-to-all-start.1 = ((bf16[32,32,256]{2,1,0:T(8,128)(2,1)}), bf16[32,32,256]{2,1,0:T(8,128)(2,1)S(1)}, u32[]{:S(2)}, u32[]{:S(2)}) async-start(bf16[32,32,256]{2,1,0:T(8,128)(2,1)} %param.12), calls=%async_computation.1 | async-start | bytes 1048576 | tf_op jit(solution)/shard_map/all_to_all | solution.py:192
  38.2 17.9 %all-to-all-start.5 = ((bf16[4,2,128]{2,1,0:T(2,128)(2,1)}), bf16[4,2,128]{2,1,0:T(2,128)(2,1)S(1)}, u32[]{:S(2)}, u32[]{:S(2)}) async-start(bf16[4,2,128]{2,1,0:T(2,128)(2,1)} %reshape.268), calls=%async_computation.5 | async-start | bytes 4096 | tf_op jit(solution)/shard_map/all_to_all | solution.py:207
  46.0 4.9 %copy-start.29 = (bf16[4,256,256]{1,2,0:T(8,128)(2,1)}, bf16[4,256,256]{1,2,0:T(8,128)(2,1)S(1)}, u32[]{:S(2)}) copy-start(bf16[4,256,256]{1,2,0:T(8,128)(2,1)S(1)} %copy.369) | copy-start | bytes 1572868
  46.2 4.7 %copy-start.8 = (bf16[4,256,256]{1,2,0:T(8,128)(2,1)}, bf16[4,256,256]{1,2,0:T(8,128)(2,1)S(1)}, u32[]{:S(2)}) copy-start(bf16[4,256,256]{1,2,0:T(8,128)(2,1)S(1)} %copy.368) | copy-start | bytes 1572868
  53.7 5.9 %copy-start.27 = (bf16[32,32,256]{2,1,0:T(8,128)(2,1)S(1)}, bf16[32,32,256]{2,1,0:T(8,128)(2,1)}, u32[]{:S(2)}) copy-start(bf16[32,32,256]{2,1,0:T(8,128)(2,1)} %param.14) | copy-start | bytes 1572868
  56.1 18.8 %all-to-all-start.3 = ((bf16[4,256,256]{2,0,1:T(4,128)(2,1)}), bf16[4,256,256]{2,0,1:T(4,128)(2,1)S(1)}, u32[]{:S(2)}, u32[]{:S(2)}) async-start(bf16[4,256,256]{2,0,1:T(4,128)(2,1)} %copy.374), calls=%async_computation.3 | async-start | bytes 1048576 | tf_op jit(solution)/shard_map/all_to_all | solution.py:199
  74.8 12.0 %all-to-all-start = ((bf16[32,32,256]{2,0,1:T(8,128)(2,1)}), bf16[32,32,256]{2,0,1:T(8,128)(2,1)S(1)}, u32[]{:S(2)}, u32[]{:S(2)}) async-start(bf16[32,32,256]{2,0,1:T(8,128)(2,1)} %copy.364), calls=%async_computation | async-start | bytes 1048576 | tf_op jit(solution)/shard_map/all_to_all | solution.py:206
  86.9 11.8 %copy-start.2 = (bf16[32,32,256]{2,0,1:T(8,128)(2,1)}, bf16[32,32,256]{2,0,1:T(8,128)(2,1)S(1)}, u32[]{:S(2)}) copy-start(bf16[32,32,256]{2,0,1:T(8,128)(2,1)S(1)} %all-to-all-done) | copy-start | bytes 1572868
  86.9 10.4 %all-to-all-start.4 = ((bf16[32,32,256]{2,0,1:T(8,128)(2,1)}), bf16[32,32,256]{2,0,1:T(8,128)(2,1)S(1)}, u32[]{:S(2)}, u32[]{:S(2)}) async-start(bf16[32,32,256]{2,0,1:T(8,128)(2,1)} %copy.377), calls=%async_computation.4 | async-start | bytes 1048576 | tf_op jit(solution)/shard_map/all_to_all | solution.py:198
  90.7 8.9 %copy-start.40 = (f32[256]{0:T(256)S(1)}, f32[256]{0:T(256)}, u32[]{:S(2)}) copy-start(f32[256]{0:T(256)} %param.18) | copy-start | bytes 3076
  107.9 5.8 %copy-start.20 = (bf16[128,8,256]{0,2,1:T(8,128)(2,1)}, bf16[128,8,256]{0,2,1:T(8,128)(2,1)S(1)}, u32[]{:S(2)}) copy-start(bf16[128,8,256]{0,2,1:T(8,128)(2,1)S(1)} %copy.385) | copy-start | bytes 1572868
  132.6 5.2 %copy-start.32 = (bf16[128,8,256]{0,2,1:T(8,128)(2,1)S(1)}, bf16[128,8,256]{0,2,1:T(8,128)(2,1)}, u32[]{:S(2)}) copy-start(bf16[128,8,256]{0,2,1:T(8,128)(2,1)} %copy.386) | copy-start | bytes 1572868
  144.1 4.3 %copy-start.31 = (bf16[128,8,256]{2,0,1:T(8,128)(2,1)}, bf16[128,8,256]{2,0,1:T(8,128)(2,1)S(1)}, u32[]{:S(2)}) copy-start(bf16[128,8,256]{2,0,1:T(8,128)(2,1)S(1)} %copy.398) | copy-start | bytes 1572868
  151.6 6.1 %copy-start.3 = (bf16[32,32,256]{2,0,1:T(8,128)(2,1)S(1)}, bf16[32,32,256]{2,0,1:T(8,128)(2,1)}, u32[]{:S(2)}) copy-start(bf16[32,32,256]{2,0,1:T(8,128)(2,1)} %copy-done.2) | copy-start | bytes 1572868
  152.5 6.3 %copy-start.11 = (bf16[4,4,64,256]{3,2,1,0:T(8,128)(2,1)S(1)}, bf16[4,4,64,256]{3,2,1,0:T(8,128)(2,1)}, u32[]{:S(2)}) copy-start(bf16[4,4,64,256]{3,2,1,0:T(8,128)(2,1)} %copy-done.10) | copy-start | bytes 1572868
  153.6 10.8 %all-to-all-start.6 = ((bf16[128,8,256]{2,1,0:T(8,128)(2,1)}), bf16[128,8,256]{2,1,0:T(8,128)(2,1)}, u32[]{:S(2)}, u32[]{:S(2)}) async-start(bf16[128,8,256]{2,1,0:T(8,128)(2,1)} %copy.399), calls=%async_computation.6 | async-start | bytes 1048576 | tf_op jit(solution)/shard_map/all_to_all | solution.py:221
  159.2 10.9 %copy-start.6 = (bf16[128,8,256]{2,0,1:T(8,128)(2,1)S(1)}, bf16[128,8,256]{2,0,1:T(8,128)(2,1)}, u32[]{:S(2)}) copy-start(bf16[128,8,256]{2,0,1:T(8,128)(2,1)} %copy-done.4) | copy-start | bytes 1572868
  163.5 8.9 %copy-start.18 = (bf16[128,8,256]{2,0,1:T(8,128)(2,1)S(1)}, bf16[128,8,256]{2,0,1:T(8,128)(2,1)}, u32[]{:S(2)}) copy-start(bf16[128,8,256]{2,0,1:T(8,128)(2,1)} %copy-done.17) | copy-start | bytes 1572868
  166.3 18.8 %all-to-all-start.7 = ((bf16[32,32,256]{2,1,0:T(8,128)(2,1)}), bf16[32,32,256]{2,1,0:T(8,128)(2,1)S(1)}, u32[]{:S(2)}, u32[]{:S(2)}) async-start(bf16[32,32,256]{2,1,0:T(8,128)(2,1)} %bitcast.239), calls=%async_computation.7 | async-start | bytes 1048576 | tf_op jit(solution)/shard_map/all_to_all | solution.py:220
  169.8 200.5 %all-reduce.4.cloned.1.call-start = ((), (), s32[]{:S(2)}) async-start(), calls=%async_computation.9 | async-start | bytes 8388608 | tf_op jit(solution)/shard_map/psum | solution.py:232
  192.0 8.0 %copy-start.30 = (bf16[4,256,256]{1,2,0:T(8,128)(2,1)S(1)}, bf16[4,256,256]{1,2,0:T(8,128)(2,1)}, u32[]{:S(2)}) copy-start(bf16[4,256,256]{1,2,0:T(8,128)(2,1)} %copy-done.29) | copy-start | bytes 1572868
  208.0 5.5 %copy-start.19 = (bf16[32,8,4,256]{3,1,2,0:T(8,128)(2,1)S(1)}, bf16[32,8,4,256]{3,1,2,0:T(8,128)(2,1)}, u32[]{:S(2)}) copy-start(bf16[32,8,4,256]{3,1,2,0:T(8,128)(2,1)} %copy.437) | copy-start | bytes 1572868
  208.0 6.5 %copy-start.16 = (bf16[4,256,256]{2,1,0:T(8,128)(2,1)S(1)}, bf16[4,256,256]{2,1,0:T(8,128)(2,1)}, u32[]{:S(2)}) copy-start(bf16[4,256,256]{2,1,0:T(8,128)(2,1)} %copy-done.15) | copy-start | bytes 1572868
  219.8 5.6 %copy-start.42 = (f32[256]{0:T(256)S(1)}, f32[256]{0:T(256)}, u32[]{:S(2)}) copy-start(f32[256]{0:T(256)} %get-tuple-element.73) | copy-start | bytes 3076
  219.8 5.6 %copy-start.43 = (f32[256]{0:T(256)S(1)}, f32[256]{0:T(256)}, u32[]{:S(2)}) copy-start(f32[256]{0:T(256)} %get-tuple-element.84) | copy-start | bytes 3076
  221.9 44.8 %all-to-all-start.8 = ((bf16[4,256,256]{2,0,1:T(4,128)(2,1)}), bf16[4,256,256]{2,0,1:T(4,128)(2,1)S(1)}, u32[]{:S(2)}, u32[]{:S(2)}) async-start(bf16[4,256,256]{2,0,1:T(4,128)(2,1)} %copy.409), calls=%async_computation.8 | async-start | bytes 1048576 | tf_op jit(solution)/shard_map/all_to_all | solution.py:230
  370.2 6.0 %copy-start.38 = (f32[256,256]{1,0:T(8,128)S(1)}, f32[256,256]{1,0:T(8,128)}, u32[]{:S(2)}) copy-start(f32[256,256]{1,0:T(8,128)} %get-tuple-element.143) | copy-start | bytes 786436
  370.2 6.7 %copy-start.24 = (f32[256,1024]{1,0:T(8,128)S(1)}, f32[256,1024]{1,0:T(8,128)}, u32[]{:S(2)}) copy-start(f32[256,1024]{1,0:T(8,128)} %get-tuple-element.145) | copy-start | bytes 3145732
  370.2 7.7 %copy-start.23 = (f32[1024,256]{1,0:T(8,128)S(1)}, f32[1024,256]{1,0:T(8,128)}, u32[]{:S(2)}) copy-start(f32[1024,256]{1,0:T(8,128)} %get-tuple-element.146) | copy-start | bytes 3145732
  372.5 6.4 %copy-start.1 = (bf16[256,1024]{1,0:T(8,128)(2,1)S(1)}, bf16[256,1024]{1,0:T(8,128)(2,1)}, u32[]{:S(2)}) copy-start(bf16[256,1024]{1,0:T(8,128)(2,1)} %param.22) | copy-start | bytes 1572868
  (23 other events, 51.3 us)
Sparse Core Ops, SparseCore 0:
  217.3 152.8 all-reduce.3
where the time goes:
time: 387 us; the launch traced here: 386 us
  waiting for transfers between devices  149 us (39%)
  matrix products  80.4 us (21%)
  blocking collectives  53.3 us (14%)
  local copies, waits for them, and re-layouts  52.3 us (14%)
  starting transfers between devices  30.1 us (8%)
  between operations  14.7 us (4%)
  other arithmetic  5.81 us (2%)
    psum x1, waiting for transfers between devices, shards(): lax.psum((row_sums[0], row_sums[1], row_sums[2], other_sums[0], other_sum...  103 us
    dot_general x10, matrix products, product(): jnp.einsum(spec_text, left_op, right_op, preferred_element_type=jnp.float32)  42.8 us
    psum x1, blocking collectives, shards(): lax.psum((row_sums[0], row_sums[1], row_sums[2], other_sums[0], other_sum...  41.2 us
    unnamed x104, local copies, waits for them, and re-layouts  17.6 us
    all_to_all x1, waiting for transfers between devices, shards(): lax.all_to_all(after_rows, 'cols', split_axis=1, concat_axis=0, tiled=True)  14.2 us
    all_to_all x1, waiting for transfers between devices, shards(): lax.all_to_all(tokens, 'cols', split_axis=0, concat_axis=1, tiled=True)  13.7 us
    dot_general x6, matrix products, over_cells(): lax.dot_general(left_flat, right_flat, (((0,), (0,)), ((), ())), preferre...  13.3 us
    all_to_all x1, blocking collectives, shards(): lax.all_to_all(key_bias, 'cols', split_axis=0, concat_axis=1, tiled=True)  12.1 us
  transfers between devices with their start and end apart: 9, of which 7 were waited for; matrix products, arithmetic and copies ran while one was open for 10% of the time, Pallas kernels for 0%

commit v1 on v0

--- a/solution.py
+++ b/solution.py
@@ -229,20 +229,19 @@
     )
     d_tokens = lax.all_to_all(token_grad_rows, "cols", split_axis=1, concat_axis=0, tiled=True)
     row_sums = tuple((grad_term * factor for grad_term in row_grads))
-    summed = lax.psum(
-        (
-            row_sums[0],
-            row_sums[1],
-            row_sums[2],
-            other_sums[0],
-            other_sums[1],
-            other_sums[2],
-            other_sums[3],
-            other_sums[4],
-            other_sums[5],
-        ),
-        ("rows", "cols"),
-    )
+    summed = (
+        row_sums[0],
+        row_sums[1],
+        row_sums[2],
+        other_sums[0],
+        other_sums[1],
+        other_sums[2],
+        other_sums[3],
+        other_sums[4],
+        other_sums[5],
+    )
+    for q in ("cols", "rows"):
+        summed = lax.psum(summed, q)
     row_sums = summed[:3]
     other_sums = summed[3:]
     return (

time: 387 us -> 442 us (1.14)
  waiting for transfers between devices: 149 us -> 214 us
  blocking collectives: 53.3 us -> 43.4 us
    psum x1 -> x2, waiting for transfers between devices: 103 us -> 168 us  [shards(): summed = lax.psum(summed, q)]
    psum x1 -> x2, blocking collectives: 41.2 us -> 31.4 us  [shards(): summed = lax.psum(summed, q)]
  transfers between devices with their start and end apart: 9 -> 10, of which waited for: 7 -> 8; matrix products, arithmetic and copies ran while one was open for 10% -> 8% of each run, Pallas kernels for 0% -> 0%
where the time goes in v1:
time: 442 us; the launch traced here: 440 us
  waiting for transfers between devices  214 us (48%)
  matrix products  80.5 us (18%)
  local copies, waits for them, and re-layouts  51 us (12%)
  blocking collectives  43.4 us (10%)
  starting transfers between devices  30.5 us (7%)
  between operations  14.7 us (3%)
  other arithmetic  5.81 us (1%)
    psum x2, waiting for transfers between devices, shards(): summed = lax.psum(summed, q)  168 us
    dot_general x10, matrix products, product(): jnp.einsum(spec_text, left_op, right_op, preferred_element_type=jnp.float32)  43 us
    psum x2, blocking collectives, shards(): summed = lax.psum(summed, q)  31.4 us
    unnamed x104, local copies, waits for them, and re-layouts  16.3 us
    all_to_all x1, waiting for transfers between devices, shards(): lax.all_to_all(after_rows, 'cols', split_axis=1, concat_axis=0, tiled=True)  14.2 us
    all_to_all x1, waiting for transfers between devices, shards(): lax.all_to_all(tokens, 'cols', split_axis=0, concat_axis=1, tiled=True)  13.7 us
    dot_general x6, matrix products, over_cells(): lax.dot_general(left_flat, right_flat, (((0,), (0,)), ((), ())), preferre...  13.3 us
    all_to_all x1, blocking collectives, shards(): lax.all_to_all(key_bias, 'cols', split_axis=0, concat_axis=1, tiled=True)  12.1 us
  transfers between devices with their start and end apart: 10, of which 8 were waited for; matrix products, arithmetic and copies ran while one was open for 8% of the time, Pallas kernels for 0%

profile of v1, /device:TPU:0, one launch (start us, length us, event | category | flops | bytes accessed | tf_op | source)
XLA Modules:
  0.0 440.2 jit_solution(9388503108146158370)
XLA Ops:
  7.2 12.1 %all_to_all.134 = bf16[8,4,32]{2,1,0:T(4,128)(2,1)S(1)} all-to-all(bf16[8,4,32]{2,1,0:T(4,128)(2,1)} %bitcast.263), channel_id=1, replica_groups=mesh['rows'=4,'cols'=8] {'cols'}, dimensions={0} | all-to-all | bytes 4096 | tf_op jit(solution)/shard_map/all_to_all | solution.py:193
  19.3 3.6 all-to-all-start.1
  24.4 13.7 %all-to-all-done.1 = bf16[32,32,256]{2,1,0:T(8,128)(2,1)S(1)} async-done(((bf16[32,32,256]{2,1,0:T(8,128)(2,1)}), bf16[32,32,256]{2,1,0:T(8,128)(2,1)S(1)}, u32[]{:S(2)}, u32[]{:S(2)}) %all-to-all-start.1) | async-done | bytes 524320 | tf_op jit(solution)/shard_map/all_to_all | solution.py:192
  38.2 3.7 all-to-all-start.5
  46.3 4.7 %fusion.124 = (f32[4,4,256]{2,1,0:T(4,128)S(1)}, f32[4,4,256,256]{2,3,1,0:T(8,128)}) fusion(f32[4,256]{1,0:T(4,128)S(1)} %reshape.252, bf16[4,256,4,64]{1,3,2,0:T(8,128)(2,1)S(1)} %bitcast.249, bf16[4,256,4,64]{1,3,2,0:T(8,128)(2,1)} %bitcast.247), kind=kOutput, calls=%fused_computation.165 | convolution fusion | flops 138412288 | bytes 5263360 | tf_op jit(solution)/shard_map/while/body/eval_jaxpr/sub | solution.py:72
  51.0 2.7 convolution_convert_fusion.7
  56.1 3.5 all-to-all-start.3
  60.7 14.2 %all-to-all-done.3 = bf16[4,256,256]{2,0,1:T(4,128)(2,1)S(1)} async-done(((bf16[4,256,256]{2,0,1:T(4,128)(2,1)}), bf16[4,256,256]{2,0,1:T(4,128)(2,1)S(1)}, u32[]{:S(2)}, u32[]{:S(2)}) %all-to-all-start.3) | async-done | bytes 524320 | tf_op jit(solution)/shard_map/all_to_all | solution.py:199
  74.8 4.2 all-to-all-start
  80.2 6.6 %all-to-all-done = bf16[32,32,256]{2,0,1:T(8,128)(2,1)S(1)} async-done(((bf16[32,32,256]{2,0,1:T(8,128)(2,1)}), bf16[32,32,256]{2,0,1:T(8,128)(2,1)S(1)}, u32[]{:S(2)}, u32[]{:S(2)}) %all-to-all-start) | async-done | bytes 524320 | tf_op jit(solution)/shard_map/all_to_all | solution.py:206
  86.9 3.7 all-to-all-start.4
  91.5 5.8 %all-to-all-done.4 = bf16[32,32,256]{2,0,1:T(8,128)(2,1)S(1)} async-done(((bf16[32,32,256]{2,0,1:T(8,128)(2,1)}), bf16[32,32,256]{2,0,1:T(8,128)(2,1)S(1)}, u32[]{:S(2)}, u32[]{:S(2)}) %all-to-all-start.4) | async-done | bytes 524320 | tf_op jit(solution)/shard_map/all_to_all | solution.py:198
  107.9 3.7 fusion.125
  115.3 2.8 multiply_convert_fusion
  118.2 3.2 fusion.10
  127.3 3.5 convolution_convert_fusion.5
  132.6 5.3 %fusion.42 = bf16[8,4,64,128]{3,2,1,0:T(8,128)(2,1)} fusion(bf16[128,8,4,64]{0,3,2,1:T(8,128)(2,1)} %bitcast.252, f32[8,4,128,128]{2,3,1,0:T(8,128)} %fusion.126, f32[8,4,128,128]{2,3,1,0:T(8,128)} %get-tuple-element.136, f32[8,4,128]{2,1,0:T(4,128)S(1)} %get-tuple-element.135), kind=kOutput, calls=%fused_computation.49 | convolution fusion | flops 71045248 | bytes 5259264 | tf_op jit(solution)/shard_map/while/body/eval_jaxpr/shqk,kshd->qshd/dot_general | solution.py:10
  137.9 5.0 %fusion.45 = bf16[8,4,64,128]{3,2,1,0:T(8,128)(2,1)} fusion(bf16[128,8,4,64]{0,3,2,1:T(8,128)(2,1)S(1)} %bitcast.254, f32[8,4,128,128]{2,3,1,0:T(8,128)} %fusion.126, f32[8,4,128,128]{2,3,1,0:T(8,128)} %get-tuple-element.136, f32[8,4,128]{2,1,0:T(4,128)S(1)} %get-tuple-element.135), kind=kOutput, calls=%fused_computation.50 | convolution fusion | flops 71045248 | bytes 5259264 | tf_op jit(solution)/shard_map/while/body/eval_jaxpr/shqk,qshd->kshd/dot_general | solution.py:10
  148.5 3.2 multiply_reduce_fusion.2
  153.6 4.1 all-to-all-start.6
  166.3 3.5 all-to-all-start.7
  172.4 3.0 fusion.56
  179.8 5.3 %all-to-all-done.7 = bf16[32,32,256]{2,1,0:T(8,128)(2,1)S(1)} async-done(((bf16[32,32,256]{2,1,0:T(8,128)(2,1)}), bf16[32,32,256]{2,1,0:T(8,128)(2,1)S(1)}, u32[]{:S(2)}, u32[]{:S(2)}) %all-to-all-start.7) | async-done | bytes 524320 | tf_op jit(solution)/shard_map/all_to_all | solution.py:220
  185.5 3.8 convolution_convert_fusion.4
  189.3 2.7 fusion.127
  192.0 8.1 %fusion.48 = bf16[4,4,64,256]{3,2,1,0:T(8,128)(2,1)} fusion(bf16[4,256,4,64]{1,3,2,0:T(8,128)(2,1)S(1)} %bitcast.248, f32[4,4,256,256]{2,3,1,0:T(8,128)} %fusion.127, f32[4,4,256,256]{2,3,1,0:T(8,128)} %get-tuple-element.134, f32[4,4,256]{2,1,0:T(4,128)S(1)} %get-tuple-element.133), kind=kOutput, calls=%fused_computation.51 | convolution fusion | flops 141824256 | bytes 9453568 | tf_op jit(solution)/shard_map/while/body/eval_jaxpr/shqk,skhd->sqhd/dot_general | solution.py:10
  200.1 8.0 %fusion.51 = bf16[4,4,64,256]{3,2,1,0:T(8,128)(2,1)} fusion(bf16[4,256,4,64]{1,3,2,0:T(8,128)(2,1)S(1)} %bitcast.250, f32[4,4,256,256]{2,3,1,0:T(8,128)} %fusion.127, f32[4,4,256,256]{2,3,1,0:T(8,128)} %get-tuple-element.134, f32[4,4,256]{2,1,0:T(4,128)S(1)} %get-tuple-element.133), kind=kOutput, calls=%fused_computation.52 | convolution fusion | flops 141824256 | bytes 9453568 | tf_op jit(solution)/shard_map/while/body/eval_jaxpr/shqk,sqhd->skhd/dot_general | solution.py:10
  217.3 96.9 %all-reduce.7.cloned.1.call-done = (f32[256,768]{1,0:T(8,128)}, f32[256,256]{1,0:T(8,128)}, f32[256,768]{1,0:T(8,128)}, f32[256,256]{1,0:T(8,128)}, f32[256,1024]{1,0:T(8,128)}, /*index=5*/f32[1024,256]{1,0:T(8,128)}) async-done(((f32[256,768]{1,0:T(8,128)}, f32[256,256]{1,0:T(8,128)}, f32[256,768]{1,0:T(8,128)}, f32[256,256]{1,0:T(8,128)}, f32[256,1024]{1,0:T(8,128)}, /*index=5*/f32[1024,256]{1,0:T(8,128)}), ...) | async-done | bytes 4194320 | tf_op jit(solution)/shard_map/psum | solution.py:244
  317.7 3.8 all-to-all-start.8
  321.6 20.9 %all-reduce = (f32[256]{0:T(256)S(1)}, f32[256]{0:T(256)S(1)}, f32[256]{0:T(256)S(1)}) all-reduce(f32[256]{0:T(256)S(1)} %broadcast_multiply_fusion.11, f32[256]{0:T(256)S(1)} %broadcast_multiply_fusion.10, f32[256]{0:T(256)S(1)} %broadcast_multiply_fusion.9), channel_id=1, replica_groups=mesh['rows'=4,'cols'=8] {'cols'}, use_global_device_ids=true, to_apply=%region_19.20 | all-reduce | flops 768 | bytes 6144 | tf_op jit(solution)/shard_map/psum | solution.py:244
  342.5 10.5 %all-reduce.2 = (f32[256]{0:T(256)}, f32[256]{0:T(256)}, f32[256]{0:T(256)}) all-reduce(f32[256]{0:T(256)S(1)} %get-tuple-element.91, f32[256]{0:T(256)S(1)} %get-tuple-element.92, f32[256]{0:T(256)S(1)} %get-tuple-element.102), channel_id=1, replica_groups=mesh['rows'=4,'cols'=8] {'rows'}, use_global_device_ids=true, to_apply=%region_20.21 | all-reduce | flops 768 | bytes 6144 | tf_op jit(solution)/shard_map/psum | solution.py:244
  353.9 70.8 %all-reduce.9.cloned.1.call-done = (f32[256,768]{1,0:T(8,128)}, f32[256,256]{1,0:T(8,128)}, f32[256,768]{1,0:T(8,128)}, f32[256,256]{1,0:T(8,128)}, f32[256,1024]{1,0:T(8,128)}, /*index=5*/f32[1024,256]{1,0:T(8,128)}) async-done(((f32[256,768]{1,0:T(8,128)}, f32[256,256]{1,0:T(8,128)}, f32[256,768]{1,0:T(8,128)}, f32[256,256]{1,0:T(8,128)}, f32[256,1024]{1,0:T(8,128)}, /*index=5*/f32[1024,256]{1,0:T(8,128)}), ...) | async-done | bytes 4194320 | tf_op jit(solution)/shard_map/psum | solution.py:244
  (198 shorter events, 78.9 us)
Async XLA Ops:
  7.2 108.1 %copy-start = (bf16[256,1024]{1,0:T(8,128)(2,1)S(1)}, bf16[256,1024]{1,0:T(8,128)(2,1)}, u32[]{:S(2)}) copy-start(bf16[256,1024]{1,0:T(8,128)(2,1)} %param.22) | copy-start | bytes 1572868
  19.3 23.7 %copy-start.41 = (f32[256]{0:T(256)S(1)}, f32[256]{0:T(256)}, u32[]{:S(2)}) copy-start(f32[256]{0:T(256)} %param.15) | copy-start | bytes 3076
  19.3 18.9 %all-to-all-start.1 = ((bf16[32,32,256]{2,1,0:T(8,128)(2,1)}), bf16[32,32,256]{2,1,0:T(8,128)(2,1)S(1)}, u32[]{:S(2)}, u32[]{:S(2)}) async-start(bf16[32,32,256]{2,1,0:T(8,128)(2,1)} %param.12), calls=%async_computation.1 | async-start | bytes 1048576 | tf_op jit(solution)/shard_map/all_to_all | solution.py:192
  38.2 17.9 %all-to-all-start.5 = ((bf16[4,2,128]{2,1,0:T(2,128)(2,1)}), bf16[4,2,128]{2,1,0:T(2,128)(2,1)S(1)}, u32[]{:S(2)}, u32[]{:S(2)}) async-start(bf16[4,2,128]{2,1,0:T(2,128)(2,1)} %reshape.268), calls=%async_computation.5 | async-start | bytes 4096 | tf_op jit(solution)/shard_map/all_to_all | solution.py:207
  53.7 5.9 %copy-start.27 = (bf16[32,32,256]{2,1,0:T(8,128)(2,1)S(1)}, bf16[32,32,256]{2,1,0:T(8,128)(2,1)}, u32[]{:S(2)}) copy-start(bf16[32,32,256]{2,1,0:T(8,128)(2,1)} %param.14) | copy-start | bytes 1572868
  56.1 18.8 %all-to-all-start.3 = ((bf16[4,256,256]{2,0,1:T(4,128)(2,1)}), bf16[4,256,256]{2,0,1:T(4,128)(2,1)S(1)}, u32[]{:S(2)}, u32[]{:S(2)}) async-start(bf16[4,256,256]{2,0,1:T(4,128)(2,1)} %copy.374), calls=%async_computation.3 | async-start | bytes 1048576 | tf_op jit(solution)/shard_map/all_to_all | solution.py:199
  74.8 12.0 %all-to-all-start = ((bf16[32,32,256]{2,0,1:T(8,128)(2,1)}), bf16[32,32,256]{2,0,1:T(8,128)(2,1)S(1)}, u32[]{:S(2)}, u32[]{:S(2)}) async-start(bf16[32,32,256]{2,0,1:T(8,128)(2,1)} %copy.364), calls=%async_computation | async-start | bytes 1048576 | tf_op jit(solution)/shard_map/all_to_all | solution.py:206
  86.9 11.8 %copy-start.2 = (bf16[32,32,256]{2,0,1:T(8,128)(2,1)}, bf16[32,32,256]{2,0,1:T(8,128)(2,1)S(1)}, u32[]{:S(2)}) copy-start(bf16[32,32,256]{2,0,1:T(8,128)(2,1)S(1)} %all-to-all-done) | copy-start | bytes 1572868
  86.9 10.4 %all-to-all-start.4 = ((bf16[32,32,256]{2,0,1:T(8,128)(2,1)}), bf16[32,32,256]{2,0,1:T(8,128)(2,1)S(1)}, u32[]{:S(2)}, u32[]{:S(2)}) async-start(bf16[32,32,256]{2,0,1:T(8,128)(2,1)} %copy.377), calls=%async_computation.4 | async-start | bytes 1048576 | tf_op jit(solution)/shard_map/all_to_all | solution.py:198
  90.7 8.9 %copy-start.40 = (f32[256]{0:T(256)S(1)}, f32[256]{0:T(256)}, u32[]{:S(2)}) copy-start(f32[256]{0:T(256)} %param.18) | copy-start | bytes 3076
  107.9 5.8 %copy-start.20 = (bf16[128,8,256]{0,2,1:T(8,128)(2,1)}, bf16[128,8,256]{0,2,1:T(8,128)(2,1)S(1)}, u32[]{:S(2)}) copy-start(bf16[128,8,256]{0,2,1:T(8,128)(2,1)S(1)} %copy.385) | copy-start | bytes 1572868
  151.7 6.1 %copy-start.3 = (bf16[32,32,256]{2,0,1:T(8,128)(2,1)S(1)}, bf16[32,32,256]{2,0,1:T(8,128)(2,1)}, u32[]{:S(2)}) copy-start(bf16[32,32,256]{2,0,1:T(8,128)(2,1)} %copy-done.2) | copy-start | bytes 1572868
  152.5 6.3 %copy-start.11 = (bf16[4,4,64,256]{3,2,1,0:T(8,128)(2,1)S(1)}, bf16[4,4,64,256]{3,2,1,0:T(8,128)(2,1)}, u32[]{:S(2)}) copy-start(bf16[4,4,64,256]{3,2,1,0:T(8,128)(2,1)} %copy-done.10) | copy-start | bytes 1572868
  153.6 10.8 %all-to-all-start.6 = ((bf16[128,8,256]{2,1,0:T(8,128)(2,1)}), bf16[128,8,256]{2,1,0:T(8,128)(2,1)}, u32[]{:S(2)}, u32[]{:S(2)}) async-start(bf16[128,8,256]{2,1,0:T(8,128)(2,1)} %copy.399), calls=%async_computation.6 | async-start | bytes 1048576 | tf_op jit(solution)/shard_map/all_to_all | solution.py:221
  159.3 10.9 %copy-start.6 = (bf16[128,8,256]{2,0,1:T(8,128)(2,1)S(1)}, bf16[128,8,256]{2,0,1:T(8,128)(2,1)}, u32[]{:S(2)}) copy-start(bf16[128,8,256]{2,0,1:T(8,128)(2,1)} %copy-done.4) | copy-start | bytes 1572868
  163.5 8.9 %copy-start.18 = (bf16[128,8,256]{2,0,1:T(8,128)(2,1)S(1)}, bf16[128,8,256]{2,0,1:T(8,128)(2,1)}, u32[]{:S(2)}) copy-start(bf16[128,8,256]{2,0,1:T(8,128)(2,1)} %copy-done.17) | copy-start | bytes 1572868
  166.3 18.8 %all-to-all-start.7 = ((bf16[32,32,256]{2,1,0:T(8,128)(2,1)}), bf16[32,32,256]{2,1,0:T(8,128)(2,1)S(1)}, u32[]{:S(2)}, u32[]{:S(2)}) async-start(bf16[32,32,256]{2,1,0:T(8,128)(2,1)} %bitcast.239), calls=%async_computation.7 | async-start | bytes 1048576 | tf_op jit(solution)/shard_map/all_to_all | solution.py:220
  169.8 144.5 %all-reduce.7.cloned.1.call-start = ((), (), s32[]{:S(2)}) async-start(), calls=%async_computation.9 | async-start | bytes 8388608 | tf_op jit(solution)/shard_map/psum | solution.py:244
  192.0 8.1 %copy-start.30 = (bf16[4,256,256]{1,2,0:T(8,128)(2,1)S(1)}, bf16[4,256,256]{1,2,0:T(8,128)(2,1)}, u32[]{:S(2)}) copy-start(bf16[4,256,256]{1,2,0:T(8,128)(2,1)} %copy-done.29) | copy-start | bytes 1572868
  208.1 5.4 %copy-start.19 = (bf16[32,8,4,256]{3,1,2,0:T(8,128)(2,1)S(1)}, bf16[32,8,4,256]{3,1,2,0:T(8,128)(2,1)}, u32[]{:S(2)}) copy-start(bf16[32,8,4,256]{3,1,2,0:T(8,128)(2,1)} %copy.437) | copy-start | bytes 1572868
  208.1 6.4 %copy-start.16 = (bf16[4,256,256]{2,1,0:T(8,128)(2,1)S(1)}, bf16[4,256,256]{2,1,0:T(8,128)(2,1)}, u32[]{:S(2)}) copy-start(bf16[4,256,256]{2,1,0:T(8,128)(2,1)} %copy-done.15) | copy-start | bytes 1572868
  217.3 97.0 %copy-start.31 = (bf16[4,256,256]{2,1,0:T(8,128)(2,1)S(1)}, bf16[4,256,256]{2,1,0:T(8,128)(2,1)}, u32[]{:S(2)}) copy-start(bf16[4,256,256]{2,1,0:T(8,128)(2,1)} %copy.406) | copy-start | bytes 1572868
  217.3 97.0 %copy-start.33 = (bf16[4,256,256]{2,1,0:T(8,128)(2,1)S(1)}, bf16[4,256,256]{2,1,0:T(8,128)(2,1)}, u32[]{:S(2)}) copy-start(bf16[4,256,256]{2,1,0:T(8,128)(2,1)} %copy.405) | copy-start | bytes 1572868
  217.3 97.0 %copy-start.37 = (bf16[256,768]{1,0:T(8,128)(2,1)S(1)}, bf16[256,768]{1,0:T(8,128)(2,1)}, u32[]{:S(2)}) copy-start(bf16[256,768]{1,0:T(8,128)(2,1)} %param.16) | copy-start | bytes 1179652
  217.3 207.4 %all-reduce.9.cloned.1.call-start = ((), (), s32[]{:S(2)}) async-start(), calls=%async_computation.10 | async-start | bytes 8388608 | tf_op jit(solution)/shard_map/psum | solution.py:244
  315.7 5.9 %copy-start.42 = (f32[256]{0:T(256)S(1)}, f32[256]{0:T(256)}, u32[]{:S(2)}) copy-start(f32[256]{0:T(256)} %get-tuple-element.73) | copy-start | bytes 3076
  315.7 5.9 %copy-start.43 = (f32[256]{0:T(256)S(1)}, f32[256]{0:T(256)}, u32[]{:S(2)}) copy-start(f32[256]{0:T(256)} %get-tuple-element.84) | copy-start | bytes 3076
  317.7 35.2 %all-to-all-start.8 = ((bf16[4,256,256]{2,0,1:T(4,128)(2,1)}), bf16[4,256,256]{2,0,1:T(4,128)(2,1)S(1)}, u32[]{:S(2)}, u32[]{:S(2)}) async-start(bf16[4,256,256]{2,0,1:T(4,128)(2,1)} %copy.409), calls=%async_computation.8 | async-start | bytes 1048576 | tf_op jit(solution)/shard_map/all_to_all | solution.py:230
  424.7 6.0 %copy-start.38 = (f32[256,256]{1,0:T(8,128)S(1)}, f32[256,256]{1,0:T(8,128)}, u32[]{:S(2)}) copy-start(f32[256,256]{1,0:T(8,128)} %get-tuple-element.152) | copy-start | bytes 786436
  424.7 6.7 %copy-start.24 = (f32[256,1024]{1,0:T(8,128)S(1)}, f32[256,1024]{1,0:T(8,128)}, u32[]{:S(2)}) copy-start(f32[256,1024]{1,0:T(8,128)} %get-tuple-element.154) | copy-start | bytes 3145732
  424.7 7.7 %copy-start.23 = (f32[1024,256]{1,0:T(8,128)S(1)}, f32[1024,256]{1,0:T(8,128)}, u32[]{:S(2)}) copy-start(f32[1024,256]{1,0:T(8,128)} %get-tuple-element.155) | copy-start | bytes 3145732
  426.9 6.4 %copy-start.1 = (bf16[256,1024]{1,0:T(8,128)(2,1)S(1)}, bf16[256,1024]{1,0:T(8,128)(2,1)}, u32[]{:S(2)}) copy-start(bf16[256,1024]{1,0:T(8,128)(2,1)} %param.22) | copy-start | bytes 1572868
  (24 other events, 67.0 us)
Sparse Core Ops, SparseCore 0:
  217.4 96.8 all-reduce.6
  318.5 106.0 all-reduce.8
